TPU v7x, 256 devices: a whole 4x4x8 slice. The times are simulated.
256 devices in a mesh: req: 64 (over x, z, core), tp: 4 (over y).
Axes of the slice: x: 4, y: 4, z: 8, core: 2. Of those that a mesh axis runs over, the one named last changes fastest.
Arguments:
- hidden_in: bfloat16 [512, 1600], P('req'), may hold values from -6 to 6
- norm_gain: float32 [1600], replicated, may hold values from 0.1 to 1.9
- query_weight: bfloat16 [1600, 1280], P(None, 'tp'), may hold values from -0.15625 to 0.15625
- memory_weight: bfloat16 [1600, 512], P(None, 'tp'), may hold values from -0.15625 to 0.15625
- attention_out: bfloat16 [1280, 1600], P('tp'), may hold values from -0.15625 to 0.15625
- attention_gain: float32 [1280], P('tp'), may hold values from 0.1 to 1.9
- mamba_input: bfloat16 [2, 1600, 1600], P(None, None, 'tp'), may hold values from -0.15625 to 0.15625
- conv_weight: float32 [4, 1600], P(None, 'tp'), may hold values from -3 to 3
- conv_state: bfloat16 [512, 3, 1600], P('req', None, 'tp'), may hold values from -6 to 6
- select_weight: bfloat16 [1600, 132], P('tp'), may hold values from -0.15625 to 0.15625
- step_weight: bfloat16 [100, 1600], P(None, 'tp'), may hold values from -0.625 to 0.625
- step_bias: float32 [1600], P('tp'), may hold values from -4 to -1
- decay_log: float32 [16, 1600], P(None, 'tp'), may hold values from 0 to 2.77
- skip_gain: float32 [1600], P('tp'), may hold values from 0.5 to 1.5
- scan_state: float32 [512, 16, 1600], P('req', None, 'tp'), may hold values from -6 to 6
- mamba_gain: float32 [1600], P('tp'), may hold values from 0.1 to 1.9
- mamba_out: bfloat16 [1600, 1600], P('tp'), may hold values from -0.15625 to 0.15625
- cache_blocks: bfloat16 [2176, 4, 512, 128], P('req', 'tp'), as said below
- lengths: int32 [512], replicated, may hold values from 257 to 8192, as said below
- slot_request: int32 [2176], P('req'), may hold values from -1 to 511, as said below
- slot_block: int32 [2176], P('req'), may hold values from 0 to 15, as said below
Outputs:
- layer_out: bfloat16 [512, 1600], P('req', 'tp')
- new_state: float32 [512, 16, 1600], P('req', None, 'tp')
Inputs may be any that keep to these rules, and one draw needn't show every extreme that they name: `lengths`: some request holds exactly 8192 tokens. `slot_request`: -1 marks an empty slot; a request with L cached tokens fills exactly ceil(L / 512) slots; the slots of one index of req hold at most 2 blocks of the requests of any one index of req (requests r with equal r // 8), and some index of req holds exactly 2. `slot_block`: the slots of one request carry its block numbers 0 to ceil(L / 512) - 1, each once; empty slots carry 0. `cache_blocks`: the first 64 entries of the last dimension are keys, the rest values.
All inputs are finite; a program needn't handle non-finite values.
Results may differ from a plain program's by a relative error of at most 0.012.
Values may be sent and summed in bfloat16 or wider, within the bound.
A program may use at most 64 MiB of HBM per device.

v0:
```python
import jax
import jax.numpy as jnp
from jax import lax
from jax.sharding import PartitionSpec as P

HQ = 20
HD = 64
MI = 1600


def rotate_pairs(vector, position):
    head_dim = vector.shape[-1]
    half_dim = head_dim // 2
    frequency = jnp.power(
        jnp.float32(10000.0), -jnp.arange(half_dim, dtype=jnp.float32) * (2.0 / head_dim)
    )
    angles = position.astype(jnp.float32)[:, None, None] * frequency
    cosine = jnp.cos(angles)
    sine_part = jnp.sin(angles)
    front_half = vector[..., :half_dim]
    back_half = vector[..., half_dim:]
    return jnp.concatenate(
        [front_half * cosine - back_half * sine_part, back_half * cosine + front_half * sine_part],
        -1,
    )


def body(
    hidden_in,
    norm_gain,
    query_weight,
    memory_weight,
    attention_out,
    attention_gain,
    mamba_input,
    conv_weight,
    conv_state,
    select_weight,
    step_weight,
    step_bias,
    decay_log,
    skip_gain,
    scan_state,
    mamba_gain,
    mamba_out,
    cache_blocks,
    lengths,
    slot_request,
    slot_block,
):
    row_count = hidden_in.shape[0]
    model_width = hidden_in.shape[1]
    head_dim = cache_blocks.shape[3] // 2
    head_count = query_weight.shape[1] // head_dim
    block_len = cache_blocks.shape[2]
    slot_count = cache_blocks.shape[0]
    request_count = lengths.shape[0]
    holders = lax.axis_size("req")
    tp_count = lax.axis_size("tp")
    own_first = lax.axis_index("req") * row_count
    own_len = lax.dynamic_slice_in_dim(lengths, own_first, row_count)
    hidden_f = hidden_in.astype(jnp.float32)
    normed = (
        hidden_f * lax.rsqrt(jnp.mean(hidden_f * hidden_f, -1, keepdims=True) + 1e-06) * norm_gain
    ).astype(jnp.bfloat16)
    query_raw = jnp.dot(normed, query_weight, preferred_element_type=jnp.float32).reshape(
        row_count, head_count, head_dim
    )
    query = rotate_pairs(query_raw, own_len).astype(jnp.bfloat16)
    memory = jnp.dot(normed, memory_weight, preferred_element_type=jnp.float32)
    key_new = rotate_pairs(memory[:, None, :head_dim], own_len).astype(jnp.bfloat16)
    value_new = memory[:, head_dim:].astype(jnp.bfloat16)
    all_query = lax.all_gather(
        query.reshape(row_count, head_count * head_dim), "req", axis=0, tiled=True
    )
    slot_used = slot_request >= 0
    owner_row = jnp.where(slot_used, slot_request, 0)
    slot_query = jnp.take(all_query, owner_row, axis=0).reshape(slot_count, head_count, head_dim)
    keys = cache_blocks[:, 0, :, :head_dim]
    values = cache_blocks[:, 0, :, head_dim:]
    valid_len = jnp.where(slot_used, jnp.take(lengths, owner_row) - slot_block * block_len, 0)
    live_mask = jnp.arange(block_len)[None, :] < valid_len[:, None]
    scores = jnp.einsum(
        "shd,std->sht", slot_query, keys, preferred_element_type=jnp.float32
    ) * head_dim ** (-0.5)
    scores = jnp.where(live_mask[:, None, :], scores, -1e30)
    block_max = jnp.max(scores, 2)
    weights = jnp.where(live_mask[:, None, :], jnp.exp(scores - block_max[..., None]), 0.0).astype(
        jnp.bfloat16
    )
    block_sum = jnp.sum(weights.astype(jnp.float32), 2)
    block_out = jnp.einsum("sht,std->shd", weights, values, preferred_element_type=jnp.float32)
    own_score = jnp.sum(query.astype(jnp.float32) * key_new.astype(jnp.float32), -1) * head_dim ** (
        -0.5
    )
    value_own = value_new.astype(jnp.float32)[:, None, :]
    owner_match = slot_request[:, None] == jnp.arange(request_count)[None, :]
    request_max = jnp.max(jnp.where(owner_match[:, :, None], block_max[:, None, :], -1e30), axis=0)
    owner_table = owner_match.astype(jnp.float32)
    rescale = jnp.exp(block_max - jnp.take(request_max, owner_row, axis=0))
    scaled_out = (block_out * rescale[..., None]).reshape(slot_count, head_count * head_dim)
    part_out = jnp.dot(owner_table.T, scaled_out, precision=lax.Precision.HIGHEST)
    part_sum = jnp.dot(owner_table.T, block_sum * rescale, precision=lax.Precision.HIGHEST)
    part_out, part_sum = (part_out, part_sum)
    got_out, got_sum, got_max = (
        lax.all_to_all(
            part_out.reshape(holders, row_count, head_count * head_dim),
            "req",
            split_axis=0,
            concat_axis=0,
            tiled=True,
        ),
        lax.all_to_all(
            part_sum.reshape(holders, row_count, head_count),
            "req",
            split_axis=0,
            concat_axis=0,
            tiled=True,
        ),
        lax.all_to_all(
            request_max.reshape(holders, row_count, head_count),
            "req",
            split_axis=0,
            concat_axis=0,
            tiled=True,
        ),
    )
    top = jnp.maximum(jnp.max(got_max, 0), own_score)
    source_weight = jnp.exp(got_max - top[None])
    numer = jnp.sum(
        got_out.reshape(holders, row_count, head_count, head_dim) * source_weight[..., None], 0
    )
    denom = jnp.sum(got_sum * source_weight, 0)
    own_weight = jnp.exp(own_score - top)
    numer = numer + own_weight[..., None] * value_own
    denom = denom + own_weight
    attention = (numer / denom[..., None]).reshape(row_count, head_count * head_dim)
    mamba_x = jnp.dot(normed, mamba_input[0], preferred_element_type=jnp.float32).astype(
        jnp.bfloat16
    )
    gate_branch = jnp.dot(normed, mamba_input[1], preferred_element_type=jnp.float32)
    taps = conv_weight.shape[0]
    conv_sum = conv_weight[taps - 1] * mamba_x.astype(jnp.float32)
    for tap_index in range(taps - 1):
        conv_sum = conv_sum + conv_weight[tap_index] * conv_state[:, tap_index].astype(jnp.float32)
    activated = jax.nn.silu(conv_sum).astype(jnp.bfloat16)
    selection = lax.psum(
        jnp.dot(activated, select_weight, preferred_element_type=jnp.float32), "tp"
    )
    rank_width = step_weight.shape[0]
    state_width = decay_log.shape[0]
    step_rank = selection[:, :rank_width].astype(jnp.bfloat16)
    input_map = selection[:, rank_width : rank_width + state_width]
    output_map = selection[:, rank_width + state_width :]
    step_size = jax.nn.softplus(
        jnp.dot(step_rank, step_weight, preferred_element_type=jnp.float32) + step_bias
    )
    active_f = activated.astype(jnp.float32)
    new_state = (
        jnp.exp(-step_size[:, None, :] * jnp.exp(decay_log)[None]) * scan_state
        + step_size[:, None, :] * input_map[:, :, None] * active_f[:, None, :]
    )
    mamba_y = (jnp.sum(output_map[:, :, None] * new_state, 1) + skip_gain * active_f) * jax.nn.silu(
        gate_branch
    )
    attn_square = jnp.sum(attention * attention, -1)
    mamba_square = jnp.sum(mamba_y * mamba_y, -1)
    attn_used = (attention * attention_gain).astype(jnp.bfloat16)
    mamba_used = (mamba_y * mamba_gain).astype(jnp.bfloat16)
    attn_proj = jnp.dot(attn_used, attention_out, preferred_element_type=jnp.float32)
    mamba_proj = jnp.dot(mamba_used, mamba_out, preferred_element_type=jnp.float32)
    attn_total, mamba_total = lax.psum((attn_square, mamba_square), "tp")
    attn_scale = jnp.sqrt(attn_total / (HQ * HD) + 1e-06)
    mamba_scale = jnp.sqrt(mamba_total / MI + 1e-06)
    partial_value = 0.5 * (attn_proj / attn_scale[:, None] + mamba_proj / mamba_scale[:, None])
    mixed = lax.psum_scatter(partial_value, "tp", scatter_dimension=1, tiled=True)
    column_width = model_width // tp_count
    residual = lax.dynamic_slice_in_dim(
        hidden_f, lax.axis_index("tp") * column_width, column_width, 1
    )
    layer_out = (residual + mixed).astype(jnp.bfloat16)
    return (layer_out, new_state)


def solution(mesh):
    return jax.shard_map(
        body,
        mesh=mesh,
        in_specs=(
            P("req", None),
            P(),
            P(None, "tp"),
            P(None, "tp"),
            P("tp", None),
            P("tp"),
            P(None, None, "tp"),
            P(None, "tp"),
            P("req", None, "tp"),
            P("tp", None),
            P(None, "tp"),
            P("tp"),
            P(None, "tp"),
            P("tp"),
            P("req", None, "tp"),
            P("tp"),
            P("tp", None),
            P("req", "tp", None, None),
            P(),
            P("req"),
            P("req"),
        ),
        out_specs=(P("req", "tp"), P("req", None, "tp")),
        check_vma=False,
    )
```

profile of v0, /device:TPU:2, one launch (start us, length us, event | category | flops | bytes accessed | tf_op | source)
XLA Modules:
  0.0 191.9 jit_solution(11031688939695422736)
XLA Ops:
  7.2 0.8 compare_and_fusion
  8.0 0.7 iota_compare_fusion
  8.7 0.9 multiply_reduce_fusion.3
  9.6 1.3 fusion.74
  10.9 0.8 dynamic-slice_convert_fusion
  11.6 0.1 multiply_cosine_fusion.1
  11.7 0.1 fusion.65
  11.9 1.7 fusion.69
  13.5 0.1 reshape.303
  13.7 0.1 multiply_subtract_fusion
  13.8 0.2 multiply_reduce_fusion.4
  14.0 0.1 convert_element_type.89
  14.0 50.3 %all_gather.3 = bf16[512,320]{1,0:T(8,128)(2,1)S(1)} all-gather(bf16[8,320]{1,0:T(8,128)(2,1)S(1)} %convert_element_type.89), channel_id=1, replica_groups=mesh['req'=64,'tp'=4] {'req'}, dimensions={0}, use_global_device_ids=true | all-gather | bytes 332800 | tf_op jit(solution)/shard_map/all_gather | solution.py:73
  64.3 0.8 gather_fusion
  65.1 0.6 gather_fusion.1
  65.8 0.1 gather.16
  65.9 0.1 iota_compare_fusion.1
  66.0 3.6 %fusion.73 = (f32[34,5]{1,0:T(8,128)S(1)}, f32[34,5,512]{2,1,0:T(8,128)S(1)}) fusion(bf16[34,1,512,128]{3,2,1,0:T(8,128)(2,1)} %param.38, bf16[34,5,64]{2,1,0:T(8,128)(2,1)S(1)} %gather.16, pred[34]{0:T(512)(128)(4,1)S(1)} %get-tuple-element.14, pred[34,512]{1,0:T(8,128)(4,1)S(1)} %iota_compare_fusion.1), kind=kOutput, calls=%fused_computation.108 | convolution fusion | flops 11412950 | bytes 4844490 | tf_op jit(solution)/shard_map/shd,std->sht/dot_general | solution.py:83
  69.6 0.1 copy.65
  69.7 0.1 select_reduce_fusion
  69.9 0.1 copy.66
  70.0 0.6 gather_fusion.2
  70.6 0.1 subtract_exponential_fusion.1
  70.7 0.3 convert_reduce_fusion
  71.0 0.2 fusion.48
  71.2 0.1 reshape.306
  71.3 0.8 copy.72
  72.1 8.1 %all-to-all-start.2 = ((f32[64,8,5]{1,2,0:T(8,128)}), f32[64,8,5]{1,2,0:T(8,128)S(1)}, u32[]{:S(2)}, u32[]{:S(2)}) async-start(f32[64,8,5]{1,2,0:T(8,128)} %copy.72), calls=%async_computation.2 | async-start | bytes 524288 | tf_op jit(solution)/shard_map/all_to_all | solution.py:113
  80.3 3.7 %fusion.20 = f32[34,5,64]{2,1,0:T(8,128)S(1)} fusion(bf16[34,1,512,128]{3,2,1,0:T(8,128)(2,1)} %param.38, f32[34,5]{1,0:T(8,128)S(1)} %subtract_exponential_fusion.1, f32[34,5,512]{2,1,0:T(8,128)S(1)} %get-tuple-element.29, f32[34,5]{1,0:T(8,128)S(1)} %get-tuple-element.28, pred[34,512]{1,0:T(8,128)(4,1)S(1)} %iota_compare_fusion.1), kind=kOutput, calls=%fused_computation.21 | convolution fusion | flops 11413120 | bytes 4866896 | tf_op jit(solution)/shard_map/sht,std->shd/dot_general | solution.py:92
  84.0 0.1 reshape.337
  84.2 1.8 fusion.75
  86.1 0.1 fusion.77
  86.2 10.8 %psum.22 = f32[8,132]{1,0:T(8,128)S(1)} all-reduce(f32[8,132]{1,0:T(8,128)S(1)} %fusion.77), channel_id=1, replica_groups=mesh['req'=64,'tp'=4] {'tp'}, use_global_device_ids=true, to_apply=%region_10.11 | all-reduce | flops 1056 | bytes 8448 | tf_op jit(solution)/shard_map/psum | solution.py:147
  97.1 1.4 fusion.41
  98.5 0.2 fusion.76
  98.7 0.1 reshape.305
  98.8 0.8 copy.67
  99.7 10.3 %all-to-all-start.1 = ((f32[64,8,5]{1,2,0:T(8,128)}), f32[64,8,5]{1,2,0:T(8,128)S(1)}, u32[]{:S(2)}, u32[]{:S(2)}) async-start(f32[64,8,5]{1,2,0:T(8,128)} %copy.67), calls=%async_computation.1 | async-start | bytes 524288 | tf_op jit(solution)/shard_map/all_to_all | solution.py:120
  110.0 0.9 multiply_reduce_fusion.1
  110.9 10.7 %all-to-all-done.1 = f32[64,8,5]{1,2,0:T(8,128)S(1)} async-done(((f32[64,8,5]{1,2,0:T(8,128)}), f32[64,8,5]{1,2,0:T(8,128)S(1)}, u32[]{:S(2)}, u32[]{:S(2)}) %all-to-all-start.1) | async-done | bytes 10272 | tf_op jit(solution)/shard_map/all_to_all | solution.py:120
  121.6 6.5 %all-to-all-start = ((f32[64,8,320]{2,1,0:T(8,128)}), f32[64,8,320]{2,1,0:T(8,128)S(1)}, u32[]{:S(2)}, u32[]{:S(2)}) async-start(f32[64,8,320]{2,1,0:T(8,128)} %fusion.41), calls=%async_computation | async-start | bytes 1572864 | tf_op jit(solution)/shard_map/all_to_all | solution.py:106
  128.2 0.1 copy.68
  128.3 1.9 %multiply_reduce_fusion.5 = (f32[8]{0:T(128)S(1)}, f32[8,400]{1,0:T(8,128)S(1)}) fusion(bf16[2,1600,400]{1,2,0:T(8,128)(2,1)} %param.27, f32[1600]{0:T(1024)S(1)} %copy-done.7, f32[8]{0:T(128)S(1)} %add_rsqrt_fusion, bf16[8,1600]{1,0:T(8,128)(2,1)S(1)} %copy-done.3, f32[8,400]{1,0:T(8,128)S(1)} %get-tuple-element.4, ...), kind=kOutput, calls=%fused_computation.61 | convolution fusion | flops 10323192 | bytes 1396864 | tf_op jit(solution)/shard_map/dot_general | solution.py:141
  130.2 0.1 reduce_max.29
  130.3 0.1 multiply_reduce_fusion.2
  130.4 0.1 copy.69
  130.5 0.1 mul.364
  130.6 1.4 copy.70
  132.0 0.1 copy.71
  132.1 0.1 broadcast_multiply_fusion
  132.2 0.1 mul.370
  132.2 0.1 copy.73
  132.3 0.1 div.48
  132.4 0.1 div.49
  132.5 17.5 %all-to-all-done = f32[64,8,320]{2,1,0:T(8,128)S(1)} async-done(((f32[64,8,320]{2,1,0:T(8,128)}), f32[64,8,320]{2,1,0:T(8,128)S(1)}, u32[]{:S(2)}, u32[]{:S(2)}) %all-to-all-start) | async-done | bytes 655392 | tf_op jit(solution)/shard_map/all_to_all | solution.py:106
  149.9 1.3 multiply_reduce_fusion
  151.2 0.1 multiply_reduce_fusion.6
  151.4 7.7 %all-reduce = (f32[8]{0:T(128)S(1)}, f32[8]{0:T(128)S(1)}) all-reduce(f32[8]{0:T(128)S(1)} %get-tuple-element.6, f32[8]{0:T(128)S(1)} %get-tuple-element.36), channel_id=1, replica_groups=mesh['req'=64,'tp'=4] {'tp'}, use_global_device_ids=true, to_apply=%region_9.10 | all-reduce | flops 16 | bytes 128 | tf_op jit(solution)/shard_map/psum | solution.py:172
  159.1 0.3 convolution_divide_fusion.1
  159.4 0.3 fusion.7
  159.7 1.2 copy.74
  160.9 22.4 %reduce-scatter.4.cloned.1.call-done = f32[400,8]{1,0:T(8,128)} async-done(((f32[1600,8]{1,0:T(8,128)}), f32[400,8]{1,0:T(8,128)}) %reduce-scatter.4.cloned.1.call-update) | async-done | bytes 12816
  183.3 1.0 copy.75
  184.3 0.7 add_convert_fusion
  (50 shorter events, 0.5 us)
Async XLA Ops:
  7.2 152.2 %copy-start = (bf16[400,1600]{1,0:T(8,128)(2,1)S(1)}, bf16[400,1600]{1,0:T(8,128)(2,1)}, u32[]{:S(2)}) copy-start(bf16[400,1600]{1,0:T(8,128)(2,1)} %param.37) | copy-start | bytes 3840004
  7.2 57.2 %copy-start.1 = (s32[512]{0:T(512)S(1)}, s32[512]{0:T(512)}, u32[]{:S(2)}) copy-start(s32[512]{0:T(512)} %param.39) | copy-start | bytes 6148
  11.9 54.0 %copy-start.10 = (s32[34]{0:T(128)S(1)}, s32[34]{0:T(128)}, u32[]{:S(2)}) copy-start(s32[34]{0:T(128)} %param.40) | copy-start | bytes 412
  11.9 54.0 %copy-start.14 = (s32[34]{0:T(128)S(1)}, s32[34]{0:T(128)}, u32[]{:S(2)}) copy-start(s32[34]{0:T(128)} %param.41) | copy-start | bytes 412
  72.1 27.5 %all-to-all-start.2 = ((f32[64,8,5]{1,2,0:T(8,128)}), f32[64,8,5]{1,2,0:T(8,128)S(1)}, u32[]{:S(2)}, u32[]{:S(2)}) async-start(f32[64,8,5]{1,2,0:T(8,128)} %copy.72), calls=%async_computation.2 | async-start | bytes 524288 | tf_op jit(solution)/shard_map/all_to_all | solution.py:113
  80.2 3.9 %copy-start.9 = (f32[4,400]{1,0:T(4,128)S(1)}, f32[4,400]{1,0:T(4,128)}, u32[]{:S(2)}) copy-start(f32[4,400]{1,0:T(4,128)} %param.28) | copy-start | bytes 19204
  80.3 3.9 %copy-start.3 = (bf16[8,1600]{1,0:T(8,128)(2,1)S(1)}, bf16[8,1600]{1,0:T(8,128)(2,1)}, u32[]{:S(2)}) copy-start(bf16[8,1600]{1,0:T(8,128)(2,1)} %param.21) | copy-start | bytes 76804
  80.3 3.9 %copy-start.7 = (f32[1600]{0:T(1024)S(1)}, f32[1600]{0:T(1024)}, u32[]{:S(2)}) copy-start(f32[1600]{0:T(1024)} %param.22) | copy-start | bytes 19204
  84.0 2.1 %copy-start.5 = (bf16[400,132]{0,1:T(8,128)(2,1)S(1)}, bf16[400,132]{0,1:T(8,128)(2,1)}, u32[]{:S(2)}) copy-start(bf16[400,132]{0,1:T(8,128)(2,1)} %param.30) | copy-start | bytes 316804
  84.1 14.3 %copy-start.6 = (bf16[100,400]{0,1:T(8,128)(2,1)S(1)}, bf16[100,400]{0,1:T(8,128)(2,1)}, u32[]{:S(2)}) copy-start(bf16[100,400]{0,1:T(8,128)(2,1)} %param.31) | copy-start | bytes 240004
  84.1 14.3 %copy-start.11 = (f32[400]{0:T(512)S(1)}, f32[400]{0:T(512)}, u32[]{:S(2)}) copy-start(f32[400]{0:T(512)} %param.32) | copy-start | bytes 4804
  84.2 15.5 %copy-start.8 = (f32[16,400]{1,0:T(8,128)S(1)}, f32[16,400]{1,0:T(8,128)}, u32[]{:S(2)}) copy-start(f32[16,400]{1,0:T(8,128)} %param.33) | copy-start | bytes 76804
  86.1 24.0 %copy-start.4 = (f32[8,16,400]{2,1,0:T(8,128)S(1)}, f32[8,16,400]{2,1,0:T(8,128)}, u32[]{:S(2)}) copy-start(f32[8,16,400]{2,1,0:T(8,128)} %param.35) | copy-start | bytes 614404
  99.7 28.6 %copy-start.15 = (f32[400]{0:T(512)S(1)}, f32[400]{0:T(512)}, u32[]{:S(2)}) copy-start(f32[400]{0:T(512)} %param.34) | copy-start | bytes 4804
  99.7 21.9 %all-to-all-start.1 = ((f32[64,8,5]{1,2,0:T(8,128)}), f32[64,8,5]{1,2,0:T(8,128)S(1)}, u32[]{:S(2)}, u32[]{:S(2)}) async-start(f32[64,8,5]{1,2,0:T(8,128)} %copy.67), calls=%async_computation.1 | async-start | bytes 524288 | tf_op jit(solution)/shard_map/all_to_all | solution.py:120
  121.6 28.4 %all-to-all-start = ((f32[64,8,320]{2,1,0:T(8,128)}), f32[64,8,320]{2,1,0:T(8,128)S(1)}, u32[]{:S(2)}, u32[]{:S(2)}) async-start(f32[64,8,320]{2,1,0:T(8,128)} %fusion.41), calls=%async_computation | async-start | bytes 1572864 | tf_op jit(solution)/shard_map/all_to_all | solution.py:106
  128.1 55.2 %reduce-scatter.4.cloned.1.call-start = ((), (), s32[]{:S(2)}) async-start(), calls=%async_computation.4 | async-start | bytes 1024000
  132.0 27.1 %copy-start.2 = (bf16[320,1600]{1,0:T(8,128)(2,1)S(1)}, bf16[320,1600]{1,0:T(8,128)(2,1)}, u32[]{:S(2)}) copy-start(bf16[320,1600]{1,0:T(8,128)(2,1)} %param.25) | copy-start | bytes 3072004
  132.0 27.1 %copy-start.12 = (f32[320]{0:T(512)S(1)}, f32[320]{0:T(512)}, u32[]{:S(2)}) copy-start(f32[320]{0:T(512)} %param.26) | copy-start | bytes 3844
  132.5 26.9 %copy-start.13 = (f32[400]{0:T(512)S(1)}, f32[400]{0:T(512)}, u32[]{:S(2)}) copy-start(f32[400]{0:T(512)} %param.36) | copy-start | bytes 4804
Sparse Core Ops, SparseCore 0:
  161.0 22.2 reduce-scatter.3
where the time goes:
time: 193 us; the launch traced here: 192 us
  blocking collectives  68.9 us (36%)
  waiting for transfers between devices  50.5 us (26%)
  starting transfers between devices  25 us (13%)
  matrix products  16.5 us (9%)
  between operations  14.4 us (7%)
  local copies, waits for them, and re-layouts  8.94 us (5%)
  other arithmetic  7.63 us (4%)
    all_gather x1, blocking collectives, body(): lax.all_gather(query.reshape(row_count, head_count * head_dim), 'req', ax...  50.3 us
    unnamed x2, waiting for transfers between devices  22.4 us
    all_to_all x1, waiting for transfers between devices, body(): lax.all_to_all(part_out.reshape(holders, row_count, head_count * head_dim...  17.5 us
    psum x1, blocking collectives, body(): lax.psum(jnp.dot(activated, select_weight, preferred_element_type=jnp.flo...  10.8 us
    all_to_all x1, waiting for transfers between devices, body(): lax.all_to_all(request_max.reshape(holders, row_count, head_count), 'req'...  10.7 us
    all_to_all x1, starting transfers between devices, body(): lax.all_to_all(request_max.reshape(holders, row_count, head_count), 'req'...  10.3 us
    all_to_all x1, starting transfers between devices, body(): lax.all_to_all(part_sum.reshape(holders, row_count, head_count), 'req', s...  8.09 us
    psum x1, blocking collectives, body(): attn_total, mamba_total = lax.psum((attn_square, mamba_square), 'tp')  7.74 us
  transfers between devices with their start and end apart: 4, of which 3 were waited for; matrix products, arithmetic and copies ran while one was open for 7% of the time, Pallas kernels for 0%

commit v1 on v0

--- a/solution.py
+++ b/solution.py
@@ -6,6 +6,12 @@
 HQ = 20
 HD = 64
 MI = 1600
+
+
+def gather_from_all(x, axis, dim):
+    length = lax.axis_size(axis)
+    repeats = [length if d == dim else 1 for d in range(x.ndim)]
+    return lax.all_to_all(jnp.tile(x, repeats), axis, split_axis=dim, concat_axis=dim, tiled=True)
 
 
 def rotate_pairs(vector, position):
@@ -70,9 +76,7 @@
     memory = jnp.dot(normed, memory_weight, preferred_element_type=jnp.float32)
     key_new = rotate_pairs(memory[:, None, :head_dim], own_len).astype(jnp.bfloat16)
     value_new = memory[:, head_dim:].astype(jnp.bfloat16)
-    all_query = lax.all_gather(
-        query.reshape(row_count, head_count * head_dim), "req", axis=0, tiled=True
-    )
+    all_query = gather_from_all(query.reshape(row_count, head_count * head_dim), "req", 0)
     slot_used = slot_request >= 0
     owner_row = jnp.where(slot_used, slot_request, 0)
     slot_query = jnp.take(all_query, owner_row, axis=0).reshape(slot_count, head_count, head_dim)

time: 193 us -> 159 us (0.82)
  blocking collectives: 68.9 us -> 18.6 us
  starting transfers between devices: 25 us -> 35.5 us
  waiting for transfers between devices: 50.5 us -> 56.8 us
    all_gather x1 -> x0, blocking collectives: 50.3 us -> none  [body(): lax.all_gather(query.reshape(row_count, head_count * head_dim), 'req', ax...]
    all_to_all x0 -> x1, starting transfers between devices: none -> 12.2 us  [gather_from_all(): lax.all_to_all(jnp.tile(x, repeats), axis, split_axis=dim, concat_axis=di...]
    all_to_all x1, waiting for transfers between devices: 0.01 us -> 6.8 us  [body(): lax.all_to_all(part_sum.reshape(holders, row_count, head_count), 'req', s...]
    all_to_all x1, starting transfers between devices: 10.3 us -> 6.49 us  [body(): lax.all_to_all(request_max.reshape(holders, row_count, head_count), 'req'...]
    all_to_all x1, starting transfers between devices: 8.09 us -> 10.3 us  [body(): lax.all_to_all(part_sum.reshape(holders, row_count, head_count), 'req', s...]
  transfers between devices with their start and end apart: 4 -> 5, of which waited for: 3 -> 4; matrix products, arithmetic and copies ran while one was open for 7% -> 9% of each run, Pallas kernels for 0% -> 0%
where the time goes in v1:
time: 159 us; the launch traced here: 158 us
  waiting for transfers between devices  56.8 us (36%)
  starting transfers between devices  35.5 us (22%)
  blocking collectives  18.6 us (12%)
  matrix products  16.5 us (10%)
  between operations  14.4 us (9%)
  local copies, waits for them, and re-layouts  9.73 us (6%)
  other arithmetic  6.36 us (4%)
    unnamed x2, waiting for transfers between devices  22.4 us
    all_to_all x1, waiting for transfers between devices, body(): lax.all_to_all(part_out.reshape(holders, row_count, head_count * head_dim...  17.5 us
    all_to_all x1, starting transfers between devices, gather_from_all(): lax.all_to_all(jnp.tile(x, repeats), axis, split_axis=dim, concat_axis=di...  12.2 us
    psum x1, blocking collectives, body(): lax.psum(jnp.dot(activated, select_weight, preferred_element_type=jnp.flo...  10.8 us
    all_to_all x1, starting transfers between devices, body(): lax.all_to_all(part_sum.reshape(holders, row_count, head_count), 'req', s...  10.3 us
    all_to_all x1, waiting for transfers between devices, body(): lax.all_to_all(request_max.reshape(holders, row_count, head_count), 'req'...  10.1 us
    psum x1, blocking collectives, body(): attn_total, mamba_total = lax.psum((attn_square, mamba_square), 'tp')  7.74 us
    all_to_all x1, waiting for transfers between devices, body(): lax.all_to_all(part_sum.reshape(holders, row_count, head_count), 'req', s...  6.8 us
  transfers between devices with their start and end apart: 5, of which 4 were waited for; matrix products, arithmetic and copies ran while one was open for 9% of the time, Pallas kernels for 0%

profile of v1, /device:TPU:2, one launch (start us, length us, event | category | flops | bytes accessed | tf_op | source)
XLA Modules:
  0.0 157.9 jit_solution(17377567592609342714)
XLA Ops:
  7.2 1.0 multiply_reduce_fusion.3
  8.2 1.3 fusion.74
  9.5 0.8 dynamic-slice_convert_fusion
  10.3 0.1 multiply_cosine_fusion.1
  10.4 0.1 fusion.65
  10.6 1.7 %fusion.69 = f32[8,320]{1,0:T(8,128)S(1)} fusion(bf16[1600,320]{0,1:T(8,128)(2,1)} %param.23, f32[1600]{0:T(1024)} %param.22, f32[8]{0:T(128)S(1)} %add_rsqrt_fusion, bf16[8,1600]{1,0:T(8,128)(2,1)} %param.21), kind=kOutput, calls=%fused_computation.104 | convolution fusion | flops 8243200 | bytes 1066272 | tf_op jit(solution)/shard_map/dot_general | solution.py:72
  12.2 0.1 reshape.312
  12.4 0.1 multiply_subtract_fusion
  12.5 0.2 multiply_reduce_fusion.4
  12.6 0.1 convert_element_type.92
  12.7 0.8 tile.2
  13.5 12.2 %all-to-all-start = ((bf16[64,8,320]{2,1,0:T(8,128)(2,1)}), bf16[64,8,320]{2,1,0:T(8,128)(2,1)S(1)}, u32[]{:S(2)}, u32[]{:S(2)}) async-start(bf16[64,8,320]{2,1,0:T(8,128)(2,1)} %tile.2), calls=%async_computation | async-start | bytes 786432 | tf_op jit(solution)/shard_map/all_to_all | solution.py:14
  25.8 0.1 iota_compare_fusion
  25.9 0.8 gather_fusion
  26.7 0.1 iota_compare_fusion.1
  26.8 1.8 %fusion.75 = (f32[8,400]{1,0:T(8,128)S(1)}, bf16[8,400]{1,0:T(8,128)(2,1)S(1)}) fusion(bf16[8,3,400]{2,0,1:T(8,128)(2,1)} %param.29, f32[400]{0:T(512)S(1)} %bitcast.83, f32[400]{0:T(512)S(1)} %bitcast.84, f32[400]{0:T(512)S(1)} %bitcast.82, bf16[2,1600,400]{1,2,0:T(8,128)(2,1)} %param.27, f32[1600]{0:T(1024)S(1)} %copy-done.7, f32[8]{0:T(128)S(1)} %add_rsqrt_fusion, ...), kind=kOutput, calls=%fused_computation.110 | convolution fusion | flops 10348800 | bytes 1413408 | tf_op jit(solution)/shard_map/dot_general | solution.py:142
  28.7 0.1 fusion.77
  28.8 10.8 %psum.22 = f32[8,132]{1,0:T(8,128)S(1)} all-reduce(f32[8,132]{1,0:T(8,128)S(1)} %fusion.77), channel_id=1, replica_groups=mesh['req'=64,'tp'=4] {'tp'}, use_global_device_ids=true, to_apply=%region_10.11 | all-reduce | flops 1056 | bytes 8448 | tf_op jit(solution)/shard_map/psum | solution.py:151
  39.8 0.2 fusion.76
  40.0 0.9 multiply_reduce_fusion.1
  40.8 0.6 gather_fusion.1
  41.5 0.1 gather.16
  41.6 3.6 %fusion.73 = (f32[34,5]{1,0:T(8,128)S(1)}, f32[34,5,512]{2,1,0:T(8,128)S(1)}) fusion(bf16[34,1,512,128]{3,2,1,0:T(8,128)(2,1)} %param.38, bf16[34,5,64]{2,1,0:T(8,128)(2,1)S(1)} %gather.16, pred[34]{0:T(512)(128)(4,1)S(1)} %get-tuple-element.14, pred[34,512]{1,0:T(8,128)(4,1)S(1)} %iota_compare_fusion.1), kind=kOutput, calls=%fused_computation.108 | convolution fusion | flops 11412950 | bytes 4844490 | tf_op jit(solution)/shard_map/shd,std->sht/dot_general | solution.py:87
  45.2 0.1 copy.65
  45.3 0.1 select_reduce_fusion
  45.5 0.1 copy.66
  45.6 0.6 gather_fusion.2
  46.2 0.1 subtract_exponential_fusion.1
  46.3 0.3 convert_reduce_fusion
  46.6 0.2 fusion.48
  46.8 0.1 reshape.315
  46.9 0.8 copy.72
  47.7 10.3 %all-to-all-start.3 = ((f32[64,8,5]{1,2,0:T(8,128)}), f32[64,8,5]{1,2,0:T(8,128)S(1)}, u32[]{:S(2)}, u32[]{:S(2)}) async-start(f32[64,8,5]{1,2,0:T(8,128)} %copy.72), calls=%async_computation.3 | async-start | bytes 524288 | tf_op jit(solution)/shard_map/all_to_all | solution.py:117
  58.1 3.7 %fusion.20 = f32[34,5,64]{2,1,0:T(8,128)S(1)} fusion(bf16[34,1,512,128]{3,2,1,0:T(8,128)(2,1)} %param.38, f32[34,5]{1,0:T(8,128)S(1)} %subtract_exponential_fusion.1, f32[34,5,512]{2,1,0:T(8,128)S(1)} %get-tuple-element.29, f32[34,5]{1,0:T(8,128)S(1)} %get-tuple-element.28, pred[34,512]{1,0:T(8,128)(4,1)S(1)} %iota_compare_fusion.1), kind=kOutput, calls=%fused_computation.21 | convolution fusion | flops 11413120 | bytes 4866896 | tf_op jit(solution)/shard_map/sht,std->shd/dot_general | solution.py:96
  61.8 0.1 reshape.314
  61.9 0.8 copy.67
  62.7 0.1 reshape.346
  62.8 6.8 %all-to-all-done.3 = f32[64,8,5]{1,2,0:T(8,128)S(1)} async-done(((f32[64,8,5]{1,2,0:T(8,128)}), f32[64,8,5]{1,2,0:T(8,128)S(1)}, u32[]{:S(2)}, u32[]{:S(2)}) %all-to-all-start.3) | async-done | bytes 10272 | tf_op jit(solution)/shard_map/all_to_all | solution.py:117
  69.6 6.5 %all-to-all-start.2 = ((f32[64,8,5]{1,2,0:T(8,128)}), f32[64,8,5]{1,2,0:T(8,128)S(1)}, u32[]{:S(2)}, u32[]{:S(2)}) async-start(f32[64,8,5]{1,2,0:T(8,128)} %copy.67), calls=%async_computation.2 | async-start | bytes 524288 | tf_op jit(solution)/shard_map/all_to_all | solution.py:124
  76.1 1.4 fusion.41
  77.5 10.1 %all-to-all-done.2 = f32[64,8,5]{1,2,0:T(8,128)S(1)} async-done(((f32[64,8,5]{1,2,0:T(8,128)}), f32[64,8,5]{1,2,0:T(8,128)S(1)}, u32[]{:S(2)}, u32[]{:S(2)}) %all-to-all-start.2) | async-done | bytes 10272 | tf_op jit(solution)/shard_map/all_to_all | solution.py:124
  87.6 6.5 %all-to-all-start.1 = ((f32[64,8,320]{2,1,0:T(8,128)}), f32[64,8,320]{2,1,0:T(8,128)S(1)}, u32[]{:S(2)}, u32[]{:S(2)}) async-start(f32[64,8,320]{2,1,0:T(8,128)} %fusion.41), calls=%async_computation.1 | async-start | bytes 1572864 | tf_op jit(solution)/shard_map/all_to_all | solution.py:110
  94.3 0.1 copy.68
  94.3 1.9 %multiply_reduce_fusion.5 = (f32[8]{0:T(128)S(1)}, f32[8,400]{1,0:T(8,128)S(1)}) fusion(bf16[2,1600,400]{1,2,0:T(8,128)(2,1)} %param.27, f32[1600]{0:T(1024)S(1)} %copy-done.7, f32[8]{0:T(128)S(1)} %add_rsqrt_fusion, bf16[8,1600]{1,0:T(8,128)(2,1)S(1)} %copy-done.3, f32[8,400]{1,0:T(8,128)S(1)} %get-tuple-element.4, ...), kind=kOutput, calls=%fused_computation.61 | convolution fusion | flops 10323192 | bytes 1396864 | tf_op jit(solution)/shard_map/dot_general | solution.py:145
  96.3 0.1 reduce_max.29
  96.4 0.1 multiply_reduce_fusion.2
  96.4 0.1 copy.69
  96.6 0.1 mul.364
  96.7 1.4 copy.70
  98.1 0.1 copy.71
  98.1 0.1 broadcast_multiply_fusion
  98.2 0.1 mul.370
  98.3 0.1 copy.73
  98.4 0.1 div.49
  98.5 17.5 %all-to-all-done.1 = f32[64,8,320]{2,1,0:T(8,128)S(1)} async-done(((f32[64,8,320]{2,1,0:T(8,128)}), f32[64,8,320]{2,1,0:T(8,128)S(1)}, u32[]{:S(2)}, u32[]{:S(2)}) %all-to-all-start.1) | async-done | bytes 655392 | tf_op jit(solution)/shard_map/all_to_all | solution.py:110
  116.0 1.3 multiply_reduce_fusion
  117.3 0.1 multiply_reduce_fusion.6
  117.4 7.7 %all-reduce = (f32[8]{0:T(128)S(1)}, f32[8]{0:T(128)S(1)}) all-reduce(f32[8]{0:T(128)S(1)} %get-tuple-element.6, f32[8]{0:T(128)S(1)} %get-tuple-element.36), channel_id=1, replica_groups=mesh['req'=64,'tp'=4] {'tp'}, use_global_device_ids=true, to_apply=%region_9.10 | all-reduce | flops 16 | bytes 128 | tf_op jit(solution)/shard_map/psum | solution.py:176
  125.2 0.3 convolution_divide_fusion.1
  125.5 0.3 fusion.7
  125.7 1.2 copy.74
  127.0 22.4 %reduce-scatter.4.cloned.1.call-done = f32[400,8]{1,0:T(8,128)} async-done(((f32[1600,8]{1,0:T(8,128)}), f32[400,8]{1,0:T(8,128)}) %reduce-scatter.4.cloned.1.call-update) | async-done | bytes 12816
  149.4 1.0 copy.75
  150.4 0.7 add_convert_fusion
  (52 shorter events, 0.6 us)
Async XLA Ops:
  7.2 118.3 %copy-start = (bf16[400,1600]{1,0:T(8,128)(2,1)S(1)}, bf16[400,1600]{1,0:T(8,128)(2,1)}, u32[]{:S(2)}) copy-start(bf16[400,1600]{1,0:T(8,128)(2,1)} %param.37) | copy-start | bytes 3840004
  9.4 16.3 %copy-start.10 = (s32[34]{0:T(128)S(1)}, s32[34]{0:T(128)}, u32[]{:S(2)}) copy-start(s32[34]{0:T(128)} %param.40) | copy-start | bytes 412
  9.4 16.4 %copy-start.1 = (s32[512]{0:T(512)S(1)}, s32[512]{0:T(512)}, u32[]{:S(2)}) copy-start(s32[512]{0:T(512)} %param.39) | copy-start | bytes 6148
  10.5 16.2 %copy-start.14 = (s32[34]{0:T(128)S(1)}, s32[34]{0:T(128)}, u32[]{:S(2)}) copy-start(s32[34]{0:T(128)} %param.41) | copy-start | bytes 412
  10.5 16.3 %copy-start.9 = (f32[4,400]{1,0:T(4,128)S(1)}, f32[4,400]{1,0:T(4,128)}, u32[]{:S(2)}) copy-start(f32[4,400]{1,0:T(4,128)} %param.28) | copy-start | bytes 19204
  10.5 16.3 %copy-start.3 = (bf16[8,1600]{1,0:T(8,128)(2,1)S(1)}, bf16[8,1600]{1,0:T(8,128)(2,1)}, u32[]{:S(2)}) copy-start(bf16[8,1600]{1,0:T(8,128)(2,1)} %param.21) | copy-start | bytes 76804
  10.5 16.3 %copy-start.7 = (f32[1600]{0:T(1024)S(1)}, f32[1600]{0:T(1024)}, u32[]{:S(2)}) copy-start(f32[1600]{0:T(1024)} %param.22) | copy-start | bytes 19204
  13.5 15.2 %copy-start.5 = (bf16[400,132]{0,1:T(8,128)(2,1)S(1)}, bf16[400,132]{0,1:T(8,128)(2,1)}, u32[]{:S(2)}) copy-start(bf16[400,132]{0,1:T(8,128)(2,1)} %param.30) | copy-start | bytes 316804
  13.5 27.3 %all-to-all-start = ((bf16[64,8,320]{2,1,0:T(8,128)(2,1)}), bf16[64,8,320]{2,1,0:T(8,128)(2,1)S(1)}, u32[]{:S(2)}, u32[]{:S(2)}) async-start(bf16[64,8,320]{2,1,0:T(8,128)(2,1)} %tile.2), calls=%async_computation | async-start | bytes 786432 | tf_op jit(solution)/shard_map/all_to_all | solution.py:14
  25.7 14.0 %copy-start.8 = (f32[16,400]{1,0:T(8,128)S(1)}, f32[16,400]{1,0:T(8,128)}, u32[]{:S(2)}) copy-start(f32[16,400]{1,0:T(8,128)} %param.33) | copy-start | bytes 76804
  25.7 14.1 %copy-start.6 = (bf16[100,400]{0,1:T(8,128)(2,1)S(1)}, bf16[100,400]{0,1:T(8,128)(2,1)}, u32[]{:S(2)}) copy-start(bf16[100,400]{0,1:T(8,128)(2,1)} %param.31) | copy-start | bytes 240004
  25.7 14.1 %copy-start.11 = (f32[400]{0:T(512)S(1)}, f32[400]{0:T(512)}, u32[]{:S(2)}) copy-start(f32[400]{0:T(512)} %param.32) | copy-start | bytes 4804
  25.7 14.2 %copy-start.4 = (f32[8,16,400]{2,1,0:T(8,128)S(1)}, f32[8,16,400]{2,1,0:T(8,128)}, u32[]{:S(2)}) copy-start(f32[8,16,400]{2,1,0:T(8,128)} %param.35) | copy-start | bytes 614404
  47.7 21.9 %all-to-all-start.3 = ((f32[64,8,5]{1,2,0:T(8,128)}), f32[64,8,5]{1,2,0:T(8,128)S(1)}, u32[]{:S(2)}, u32[]{:S(2)}) async-start(f32[64,8,5]{1,2,0:T(8,128)} %copy.72), calls=%async_computation.3 | async-start | bytes 524288 | tf_op jit(solution)/shard_map/all_to_all | solution.py:117
  69.6 18.0 %all-to-all-start.2 = ((f32[64,8,5]{1,2,0:T(8,128)}), f32[64,8,5]{1,2,0:T(8,128)S(1)}, u32[]{:S(2)}, u32[]{:S(2)}) async-start(f32[64,8,5]{1,2,0:T(8,128)} %copy.67), calls=%async_computation.2 | async-start | bytes 524288 | tf_op jit(solution)/shard_map/all_to_all | solution.py:124
  76.1 18.2 %copy-start.15 = (f32[400]{0:T(512)S(1)}, f32[400]{0:T(512)}, u32[]{:S(2)}) copy-start(f32[400]{0:T(512)} %param.34) | copy-start | bytes 4804
  87.6 28.4 %all-to-all-start.1 = ((f32[64,8,320]{2,1,0:T(8,128)}), f32[64,8,320]{2,1,0:T(8,128)S(1)}, u32[]{:S(2)}, u32[]{:S(2)}) async-start(f32[64,8,320]{2,1,0:T(8,128)} %fusion.41), calls=%async_computation.1 | async-start | bytes 1572864 | tf_op jit(solution)/shard_map/all_to_all | solution.py:110
  94.1 55.2 %reduce-scatter.4.cloned.1.call-start = ((), (), s32[]{:S(2)}) async-start(), calls=%async_computation.5 | async-start | bytes 1024000
  98.0 27.1 %copy-start.2 = (bf16[320,1600]{1,0:T(8,128)(2,1)S(1)}, bf16[320,1600]{1,0:T(8,128)(2,1)}, u32[]{:S(2)}) copy-start(bf16[320,1600]{1,0:T(8,128)(2,1)} %param.25) | copy-start | bytes 3072004
  98.0 27.1 %copy-start.12 = (f32[320]{0:T(512)S(1)}, f32[320]{0:T(512)}, u32[]{:S(2)}) copy-start(f32[320]{0:T(512)} %param.26) | copy-start | bytes 3844
  98.5 26.9 %copy-start.13 = (f32[400]{0:T(512)S(1)}, f32[400]{0:T(512)}, u32[]{:S(2)}) copy-start(f32[400]{0:T(512)} %param.36) | copy-start | bytes 4804
Sparse Core Ops, SparseCore 0:
  127.1 22.2 reduce-scatter.3
